TPU v7x, 32 devices: a whole 2x2x4 slice. The times are simulated.
32 devices in a mesh: dp: 8 (over z, x), mp: 4 (over y, core).
Axes of the slice: x: 2, y: 2, z: 4, core: 2. Of those that a mesh axis runs over, the one named last changes fastest.
Arguments:
- block_in: bfloat16 [8, 2048, 1024], P('dp', 'mp'), may hold values from -6 to 6
- segment_ids: int32 [8, 2048], P('dp', 'mp'), may hold values from 0 to 15, never falling along the last dimension, each value on 1 to 1024 neighbouring positions
- first_gain: bfloat16 [1024], P(('dp', 'mp')), may hold values from 0.5 to 1.5
- in_proj: bfloat16 [1024, 3072], P(('dp', 'mp')), may hold values from -0.1875 to 0.1875
- conv_kernel: bfloat16 [1024, 3], P(('dp', 'mp')), may hold values from -3 to 3
- out_proj: bfloat16 [1024, 1024], P(('dp', 'mp')), may hold values from -0.1875 to 0.1875
- second_gain: bfloat16 [1024], P(('dp', 'mp')), may hold values from 0.5 to 1.5
- gate_proj: bfloat16 [1024, 4608], P(None, 'mp'), may hold values from -0.1875 to 0.1875
- up_proj: bfloat16 [1024, 4608], P(None, 'mp'), may hold values from -0.1875 to 0.1875
- down_proj: bfloat16 [4608, 1024], P('mp'), may hold values from -0.125 to 0.125
- out_grad: bfloat16 [8, 2048, 1024], P('dp', 'mp'), may hold values from -6 to 6
Outputs:
- layer_out: bfloat16 [8, 2048, 1024], P('dp', 'mp')
- input_grad: float32 [8, 2048, 1024], P('dp', 'mp')
- grad_first: float32 [1024], P(('dp', 'mp'))
- grad_in: float32 [1024, 3072], P(('dp', 'mp'))
- grad_conv: float32 [1024, 3], P(('dp', 'mp'))
- grad_out: float32 [1024, 1024], P(('dp', 'mp'))
- grad_second: float32 [1024], P(('dp', 'mp'))
- grad_gate: float32 [1024, 4608], P(None, 'mp')
- grad_up: float32 [1024, 4608], P(None, 'mp')
- grad_down: float32 [4608, 1024], P('mp')
Inputs may be any that keep to these rules, and one draw needn't show every extreme that they name: `segment_ids`: along each sequence the ids never fall and each document is one run of positions; the longest document has exactly 1024 tokens.
All inputs are finite; a program needn't handle non-finite values.
Results may differ from a plain program's by a relative error of at most 0.013.
Values may be sent and summed in bfloat16 or wider, within the bound.
No kernel may reach another device: no remote copies, remote signals or barrier semaphores. Data moves between devices by JAX's collectives and lax.ppermute only.
A program may use at most 192 MiB of HBM per device.

v0:
```python
import jax
import jax.numpy as jnp
from jax import lax
from jax.sharding import PartitionSpec as P

KERNEL = 3
epsilon = 1e-05


def from_behind(block, axis, distance):
    devices = range(lax.axis_size(axis))
    route = [(i - distance, i) for i in devices if i - distance in devices]
    return lax.ppermute(block, axis, route)


def rms_norm(values, scale):
    return values * lax.rsqrt(jnp.mean(values * values, axis=-1, keepdims=True) + epsilon) * scale


def swiglu(gate_val, up_val):
    return jax.nn.silu(gate_val) * up_val


def inner_rows(left, right):
    return lax.dot_general(
        left, right, (((0,), (0,)), ((), ())), preferred_element_type=jnp.float32
    )


def inner_cols(left, right):
    return lax.dot_general(
        left, right, (((1,), (1,)), ((), ())), preferred_element_type=jnp.float32
    )


def causal_conv(product, rim_rows, own_ids, rim_ids, kernel):
    length = product.shape[0]
    extended = jnp.concatenate([rim_rows, product], 0)
    extended_ids = jnp.concatenate([rim_ids, own_ids], 0)
    summed = jnp.zeros_like(product)
    for offset in range(KERNEL):
        same = (extended_ids[offset : offset + length] == own_ids)[:, None]
        summed = (
            summed + jnp.where(same, extended[offset : offset + length], 0.0) * kernel[:, offset]
        )
    return summed


def per_device(
    block_in,
    segment_ids,
    first_gain,
    in_proj,
    conv_kernel,
    out_proj,
    second_gain,
    gate_proj,
    up_proj,
    down_proj,
    out_grad,
):
    row_count = block_in.shape[1]
    features = block_in.shape[2]
    lookback = KERNEL - 1
    residual_in = block_in.reshape(row_count, features).astype(jnp.float32)
    own_ids = segment_ids.reshape(row_count).astype(jnp.float32)
    gain_one, weight_in, kernel_all, weight_out, gain_two = (
        lax.all_gather(first_gain, ("dp", "mp"), axis=0, tiled=True),
        lax.all_gather(in_proj, ("dp", "mp"), axis=0, tiled=True),
        lax.all_gather(conv_kernel, ("dp", "mp"), axis=0, tiled=True),
        lax.all_gather(out_proj, ("dp", "mp"), axis=0, tiled=True),
        lax.all_gather(second_gain, ("dp", "mp"), axis=0, tiled=True),
    )
    first_normed, first_pull = jax.vjp(rms_norm, residual_in, gain_one.astype(jnp.float32))
    first_low = first_normed.astype(jnp.bfloat16)
    mixer = jnp.dot(first_low, weight_in, preferred_element_type=jnp.float32)
    opening = mixer[:, :features]
    closing = mixer[:, features : 2 * features]
    carried = mixer[:, 2 * features :]
    product = opening * carried
    rim_rows, rim_ids = from_behind(
        (product[row_count - lookback :], own_ids[row_count - lookback :]), "mp", 1
    )

    def gated_conv(product_in, closing_in, rim_in, kernel_in):
        return closing_in * causal_conv(product_in, rim_in, own_ids, rim_ids, kernel_in)

    gated, conv_pull = jax.vjp(
        gated_conv, product, closing, rim_rows, kernel_all.astype(jnp.float32)
    )
    gated_low = gated.astype(jnp.bfloat16)
    residual = residual_in + jnp.dot(gated_low, weight_out, preferred_element_type=jnp.float32)
    second_normed, second_pull = jax.vjp(rms_norm, residual, gain_two.astype(jnp.float32))
    second_low = second_normed.astype(jnp.bfloat16)
    group_rows = lax.all_gather(second_low, "mp", axis=0, tiled=True)
    gate_val = jnp.dot(group_rows, gate_proj, preferred_element_type=jnp.float32)
    up_val = jnp.dot(group_rows, up_proj, preferred_element_type=jnp.float32)
    activated, swiglu_pull = jax.vjp(swiglu, gate_val, up_val)
    hidden = activated.astype(jnp.bfloat16)
    offset_rows = lax.axis_index("mp") * row_count
    branch_sums = lax.psum(
        jnp.dot(hidden, down_proj, preferred_element_type=jnp.float32).astype(jnp.bfloat16), "mp"
    ).astype(jnp.float32)
    branch_out = lax.dynamic_slice_in_dim(branch_sums, offset_rows, row_count, 0)
    layer_out = (residual + branch_out).astype(jnp.bfloat16).reshape(1, row_count, features)
    cotangent = out_grad.reshape(row_count, features)
    cotangent_group = lax.all_gather(cotangent, "mp", axis=0, tiled=True)
    down_local = inner_rows(hidden, cotangent_group)
    hidden_grad = inner_cols(cotangent_group, down_proj)
    gate_grad, up_grad = swiglu_pull(hidden_grad)
    gate_low = gate_grad.astype(jnp.bfloat16)
    up_low = up_grad.astype(jnp.bfloat16)
    gate_local = inner_rows(group_rows, gate_low)
    up_local = inner_rows(group_rows, up_low)
    backward_sums = lax.psum(
        (inner_cols(gate_low, gate_proj) + inner_cols(up_low, up_proj)).astype(jnp.bfloat16), "mp"
    ).astype(jnp.float32)
    normed_grad = lax.dynamic_slice_in_dim(backward_sums, offset_rows, row_count, 0)
    residual_part, second_local = second_pull(normed_grad)
    residual_grad = cotangent.astype(jnp.float32) + residual_part
    residual_low = residual_grad.astype(jnp.bfloat16)
    out_local = inner_rows(gated_low, residual_low)
    gated_grad = inner_cols(residual_low, weight_out)
    product_grad, closing_grad, rim_grad, kernel_local = conv_pull(gated_grad)
    rim_back = from_behind(rim_grad, "mp", -1)
    product_grad = product_grad + jnp.pad(rim_back, ((row_count - lookback, 0), (0, 0)))
    mixer_grad = jnp.concatenate(
        [product_grad * carried, closing_grad, product_grad * opening], 1
    ).astype(jnp.bfloat16)
    in_local = inner_rows(first_low, mixer_grad)
    first_grad = inner_cols(mixer_grad, weight_in)
    input_part, first_local = first_pull(first_grad)
    input_grad = (residual_grad + input_part).reshape(1, row_count, features)
    grad_gate, grad_up, grad_down = (
        lax.psum(gate_local.astype(jnp.bfloat16), "dp").astype(jnp.float32),
        lax.psum(up_local.astype(jnp.bfloat16), "dp").astype(jnp.float32),
        lax.psum(down_local.astype(jnp.bfloat16), "dp").astype(jnp.float32),
    )
    grad_first, grad_in, grad_conv, grad_out, grad_second = (
        lax.psum_scatter(first_local, ("dp", "mp"), scatter_dimension=0, tiled=True),
        lax.psum_scatter(in_local, ("dp", "mp"), scatter_dimension=0, tiled=True),
        lax.psum_scatter(kernel_local, ("dp", "mp"), scatter_dimension=0, tiled=True),
        lax.psum_scatter(out_local, ("dp", "mp"), scatter_dimension=0, tiled=True),
        lax.psum_scatter(second_local, ("dp", "mp"), scatter_dimension=0, tiled=True),
    )
    return (
        layer_out,
        input_grad,
        grad_first,
        grad_in,
        grad_conv,
        grad_out,
        grad_second,
        grad_gate,
        grad_up,
        grad_down,
    )


def solution(mesh):
    in_specs = (
        P("dp", "mp", None),
        P("dp", "mp"),
        P(("dp", "mp")),
        P(("dp", "mp"), None),
        P(("dp", "mp"), None),
        P(("dp", "mp"), None),
        P(("dp", "mp")),
        P(None, "mp"),
        P(None, "mp"),
        P("mp", None),
        P("dp", "mp", None),
    )
    out_specs = (
        P("dp", "mp", None),
        P("dp", "mp", None),
        P(("dp", "mp")),
        P(("dp", "mp"), None),
        P(("dp", "mp"), None),
        P(("dp", "mp"), None),
        P(("dp", "mp")),
        P(None, "mp"),
        P(None, "mp"),
        P("mp", None),
    )
    return jax.shard_map(
        per_device, mesh=mesh, in_specs=in_specs, out_specs=out_specs, check_vma=False
    )
```

profile of v0, /device:TPU:0, one launch (start us, length us, event | category | flops | bytes accessed | tf_op | source)
XLA Modules:
  0.0 1103.1 jit_solution(15660055661368846921)
XLA Ops:
  7.2 0.7 all-gather.7.cloned.1.call-update
  8.0 0.7 all-gather.9.cloned.1.call-update
  8.7 0.7 convert_element_type.89
  9.5 2.3 collective-permute-start
  11.9 0.8 dynamic-update-slice
  12.7 0.8 dynamic-update-slice.1
  13.5 41.9 %all-reduce.12 = (bf16[1024]{0:T(1024)(128)(2,1)S(1)}, bf16[1024]{0:T(1024)(128)(2,1)S(1)}) all-reduce(bf16[1024]{0:T(1024)(128)(2,1)S(1)} %dynamic-update-slice, bf16[1024]{0:T(1024)(128)(2,1)S(1)} %dynamic-update-slice.1), channel_id=1, replica_groups=mesh['dp'=8,'mp'=4] {'dp','mp'}, use_global_device_ids=true, to_apply=%add.7 | all-reduce | flops 2048 | bytes 8192
  55.4 40.8 %all-gather.1 = bf16[32,32,3]{1,2,0:T(4,128)(2,1)S(1)} all-gather(bf16[1,32,3]{1,2,0:T(4,128)(2,1)} %bitcast.74), channel_id=1, replica_groups=mesh['dp'=8,'mp'=4] {'dp','mp'}, dimensions={0}, use_global_device_ids=true | all-gather | bytes 6336 | tf_op jit(solution)/shard_map/all_gather | solution.py:70
  96.2 0.1 reshape.110
  96.3 1.5 fusion.24
  98.0 6.0 fusion.35
  104.0 0.4 slice_multiply_fusion
  104.4 2.2 collective-permute-start.1
  106.7 0.7 collective-permute-done.1
  107.4 2.5 multiply_convert_fusion.6
  110.0 31.3 %all-gather.9.cloned.1.call-done = bf16[1024,1024]{1,0:T(8,128)(2,1)} async-done(((bf16[32,1024]{1,0:T(8,128)(2,1)}), bf16[1024,1024]{1,0:T(8,128)(2,1)}) %all-gather.9.cloned.1.call-update) | async-done | bytes 2097168 | tf_op jit(solution)/shard_map/all_gather | solution.py:71
  141.3 3.3 multiply_reduce_fusion.3
  144.6 1.4 copy-done.7
  146.0 1.2 multiply_convert_fusion.5
  147.2 0.5 all-gather.13.cloned.1.call-update
  147.8 0.6 all-reduce.20.cloned.1.call-start
  148.3 32.3 %all-gather.11.cloned.1.call-done = bf16[2048,1024]{1,0:T(8,128)(2,1)} async-done(((bf16[512,1024]{1,0:T(8,128)(2,1)}), bf16[2048,1024]{1,0:T(8,128)(2,1)}) %all-gather.11.cloned.1.call-update) | async-done | bytes 4194320 | tf_op jit(solution)/shard_map/all_gather | solution.py:95
  180.7 10.6 fusion.42
  191.3 7.9 fusion.43
  199.2 17.5 %all-gather.13.cloned.1.call-done = bf16[1,2048,1024]{2,1,0:T(8,128)(2,1)} async-done(((bf16[1,512,1024]{2,1,0:T(8,128)(2,1)}), bf16[1,2048,1024]{2,1,0:T(8,128)(2,1)}) %all-gather.13.cloned.1.call-update) | async-done | bytes 4194320 | tf_op jit(solution)/shard_map/all_gather | solution.py:107
  216.6 18.2 %multiply_convert_fusion = (bf16[2048,1152]{1,0:T(8,128)(2,1)}, bf16[2048,1152]{1,0:T(8,128)(2,1)}, bf16[2048,1152]{1,0:T(8,128)(2,1)}) fusion(f32[2048,1152]{1,0:T(8,128)} %fusion.42, f32[2048,1152]{1,0:T(8,128)} %fusion.43, bf16[1152,1024]{1,0:T(8,128)(2,1)S(1)} %copy-done, bf16[1,2048,1024]{2,1,0:T(8,128)(2,1)} %all-gather.13.cloned.1.call-done), kind=kOutput, calls=%fused_computation.4 | convolution fusion | flops 4869586944 | bytes 39583744 | tf_op jit(solution)/shard_map/dot_general | solution.py:31
  234.9 7.7 fusion.44
  242.6 7.1 convolution_convert_fusion.2
  249.7 7.7 add_convert_fusion
  257.5 10.1 convolution_convert_fusion
  267.6 9.6 convolution_convert_fusion.1
  277.2 133.6 %all-reduce.20.cloned.1.call-done = (bf16[2048,1024]{1,0:T(8,128)(2,1)}, bf16[2048,1024]{1,0:T(8,128)(2,1)}) async-done(((bf16[2048,1024]{1,0:T(8,128)(2,1)}, bf16[2048,1024]{1,0:T(8,128)(2,1)}), (bf16[2048,1024]{1,0:T(8,128)(2,1)}, bf16[2048,1024]{1,0:T(8,128)(2,1)})) %all-reduce.20.cloned.1.call-update) | async-done | bytes 8388624 | tf_op jit(solution)/shard_map/psum | solution.py:101
  410.8 2.0 fusion.20
  412.9 3.4 fusion.21
  416.3 1.3 fusion.32
  417.6 1.0 copy-done.4
  418.6 0.6 copy-done.10
  419.3 3.7 multiply_reduce_fusion.1
  423.0 1.1 copy.24
  424.1 9.5 fusion.8
  433.7 1.5 copy-done.6
  435.2 4.5 fusion.30
  439.8 2.0 multiply_select_fusion.2
  441.8 1.6 collective-permute-start.2
  443.4 1.0 pad_add_fusion
  444.4 0.8 collective-permute-done.2
  445.2 0.8 multiply_convert_fusion.4
  446.0 1.0 copy-done.12
  447.0 0.3 copy-done.13
  447.3 6.8 fusion.27
  454.2 8.8 fusion.18
  463.0 40.7 %all-reduce.11 = (f32[1024]{0:T(1024)S(1)}, f32[1024]{0:T(1024)S(1)}) all-reduce(f32[1024]{0:T(1024)S(1)} %get-tuple-element.15, f32[1024]{0:T(1024)S(1)} %get-tuple-element.10), channel_id=3, replica_groups=mesh['dp'=8,'mp'=4] {'dp','mp'}, use_global_device_ids=true, to_apply=%region_7.8.clone | all-reduce | flops 2048 | bytes 16384
  503.7 0.6 dynamic-slice
  504.3 0.6 dynamic-slice.1
  504.9 3.4 fusion.23
  508.4 50.0 %reduce-scatter.10.cloned.1.call-done = f32[32,3]{1,0:T(8,128)} async-done(((f32[1024,3]{1,0:T(8,128)}), f32[32,3]{1,0:T(8,128)}) %reduce-scatter.10.cloned.1.call-update) | async-done | bytes 400
  558.4 1.4 copy.25
  559.8 235.4 %all-reduce.18.cloned.1.call-done = (bf16[1024,1152]{1,0:T(8,128)(2,1)}, bf16[1024,1152]{1,0:T(8,128)(2,1)}, bf16[1152,1024]{1,0:T(8,128)(2,1)}) async-done(((bf16[1024,1152]{1,0:T(8,128)(2,1)}, bf16[1024,1152]{1,0:T(8,128)(2,1)}, bf16[1152,1024]{1,0:T(8,128)(2,1)}), (bf16[1024,1152]{1,0:T(8,128)(2,1)}, bf16[1024,1152]{1,0:T(8,128)(2,1)}, bf16[1152,1024]{1,0:T(8,128)(2,1)})) %all-reduce.18.cloned.1.call-update) | async-done | bytes 7077904 | tf_op jit(solution)/shard_map/psum | solution.py:135
  795.2 4.3 convert_element_type.106
  799.5 2.5 convert_element_type.108
  802.0 0.1 copy-done.15
  802.1 2.7 convert_element_type.110
  804.8 133.5 %reduce-scatter.8.cloned.1.call-done = f32[32,1024]{1,0:T(8,128)} async-done(((f32[1024,1024]{1,0:T(8,128)}), f32[32,1024]{1,0:T(8,128)}) %reduce-scatter.8.cloned.1.call-update) | async-done | bytes 131088 | tf_op jit(solution)/shard_map/reduce_scatter | solution.py:143
  938.4 157.9 %reduce-scatter.6.cloned.1.call-done = f32[32,3072]{1,0:T(8,128)} async-done(((f32[1024,3072]{1,0:T(8,128)}), f32[32,3072]{1,0:T(8,128)}) %reduce-scatter.6.cloned.1.call-update) | async-done | bytes 393232 | tf_op jit(solution)/shard_map/reduce_scatter | solution.py:141
  (83 shorter events, 0.9 us)
Async XLA Ops:
  7.2 209.4 %copy-start = (bf16[1152,1024]{1,0:T(8,128)(2,1)S(1)}, bf16[1152,1024]{1,0:T(8,128)(2,1)}, u32[]{:S(2)}) copy-start(bf16[1152,1024]{1,0:T(8,128)(2,1)} %param.20) | copy-start | bytes 7077892
  7.2 90.8 %all-gather.7.cloned.1.call-start = ((), (), s32[]{:S(2)}) async-start(), calls=%async_computation.3 | async-start | bytes 6488064 | tf_op jit(solution)/shard_map/all_gather | solution.py:69
  7.9 133.4 %all-gather.9.cloned.1.call-start = ((), (), s32[]{:S(2)}) async-start(), calls=%async_computation.4 | async-start | bytes 2162688 | tf_op jit(solution)/shard_map/all_gather | solution.py:71
  8.7 172.0 %all-gather.11.cloned.1.call-start = ((), (), s32[]{:S(2)}) async-start(), calls=%async_computation.5 | async-start | bytes 5242880 | tf_op jit(solution)/shard_map/all_gather | solution.py:95
  9.5 88.4 %collective-permute-start = (f32[2]{0:T(128)S(1)}, f32[2]{0:T(128)S(1)}, u32[]{:S(2)}, u32[]{:S(2)}) collective-permute-start(f32[2]{0:T(128)S(1)} %slice_bitcast_fusion), channel_id=1, source_target_pairs={{0,1},{1,2},{2,3},{4,5},{5,6},{6,7},{8,9},{9,10},{10,11},{12,13},{... | collective-permute-start | bytes 32 | tf_op jit(solution)/shard_map/ppermute | solution.py:13
  104.0 3.5 copy-start.2
  104.4 3.1 copy-start.3
  104.4 3.0 collective-permute-start.1
  107.4 33.9 %copy-start.9 = (bf16[1,512,1024]{2,1,0:T(8,128)(2,1)S(1)}, bf16[1,512,1024]{2,1,0:T(8,128)(2,1)}, u32[]{:S(2)}) copy-start(bf16[1,512,1024]{2,1,0:T(8,128)(2,1)} %param.11) | copy-start | bytes 3145732
  144.6 1.4 copy-start.7
  147.2 69.4 %all-gather.13.cloned.1.call-start = ((), (), s32[]{:S(2)}) async-start(), calls=%async_computation.8 | async-start | bytes 5242880 | tf_op jit(solution)/shard_map/all_gather | solution.py:107
  147.8 263.1 %all-reduce.20.cloned.1.call-start = ((), (), s32[]{:S(2)}) async-start(), calls=%async_computation.11 | async-start | bytes 16777216 | tf_op jit(solution)/shard_map/psum | solution.py:101
  180.7 10.6 copy-start.17
  180.7 10.6 copy-start.20
  216.6 18.2 %copy-start.19 = (bf16[1024,1152]{1,0:T(8,128)(2,1)S(1)}, bf16[1024,1152]{1,0:T(8,128)(2,1)}, u32[]{:S(2)}) copy-start(bf16[1024,1152]{1,0:T(8,128)(2,1)} %param.18) | copy-start | bytes 7077892
  234.9 7.7 copy-start.23
  234.9 14.8 %slice-start.2 = ((s8[4718592]{0:T(1024)(128)(4,1)}), s8[4194304]{0:T(1024)(128)(4,1)S(1)}, s32[]{:S(2)}) async-start(s8[4718592]{0:T(1024)(128)(4,1)} %bitcast.75), calls=%async_computation.14 | async-start | bytes 8388608
  242.5 7.2 slice-start.3
  242.6 7.1 copy-start.21
  257.5 300.9 %reduce-scatter.10.cloned.1.call-start = ((), (), s32[]{:S(2)}) async-start(), calls=%async_computation.9 | async-start | bytes 540672
  257.5 10.1 copy-start.18
  267.6 143.3 %copy-start.8 = (f32[512,1024]{1,0:T(8,128)S(1)}, f32[512,1024]{1,0:T(8,128)}, u32[]{:S(2)}) copy-start(f32[512,1024]{1,0:T(8,128)} %copy-done.7) | copy-start | bytes 6291460
  410.8 2.0 copy-start.14
  412.9 3.4 copy-start.22
  416.3 1.3 copy-start.5
  416.3 2.3 copy-start.4
  416.3 3.0 copy-start.10
  424.1 371.1 %all-reduce.18.cloned.1.call-start = ((), (), s32[]{:S(2)}) async-start(), calls=%async_computation.10 | async-start | bytes 14155776 | tf_op jit(solution)/shard_map/psum | solution.py:135
  433.6 1.6 copy-start.6
  433.7 504.7 %reduce-scatter.8.cloned.1.call-start = ((), (), s32[]{:S(2)}) async-start(), calls=%async_computation.7 | async-start | bytes 4325376 | tf_op jit(solution)/shard_map/reduce_scatter | solution.py:143
  439.7 656.6 %reduce-scatter.6.cloned.1.call-start = ((), (), s32[]{:S(2)}) async-start(), calls=%async_computation.6 | async-start | bytes 12976128 | tf_op jit(solution)/shard_map/reduce_scatter | solution.py:141
  441.8 3.4 slice-start
  441.8 3.3 slice-start.1
  441.8 3.3 collective-permute-start.2
  444.4 3.0 copy-start.11
  446.0 1.0 copy-start.12
  446.0 1.3 copy-start.13
  795.2 4.3 copy-start.16
  799.5 2.6 copy-start.15
  802.0 294.3 %copy-start.1 = (bf16[1152,1024]{1,0:T(8,128)(2,1)S(1)}, bf16[1152,1024]{1,0:T(8,128)(2,1)}, u32[]{:S(2)}) copy-start(bf16[1152,1024]{1,0:T(8,128)(2,1)} %param.20) | copy-start | bytes 7077892
Sparse Core Ops, SparseCore 0:
  10.9 72.5 all-gather.6
  86.4 54.8 all-gather.8
  147.3 33.3 all-gather.10
  182.1 34.4 all-gather.12
  257.6 153.2 all-reduce.19
  424.2 134.1 reduce-scatter.9
  563.9 231.2 all-reduce.17
  798.0 140.2 reduce-scatter.7
  945.0 151.2 reduce-scatter.5
where the time goes:
time: 1110 us; the launch traced here: 1100 us
  waiting for transfers between devices  795 us (72%)
  blocking collectives  123 us (11%)
  matrix products  119 us (11%)
  other arithmetic  32.4 us (3%)
  between operations  14.5 us (1%)
  local copies, waits for them, and re-layouts  11.6 us (1%)
    psum x1, waiting for transfers between devices, per_device(): lax.psum(gate_local.astype(jnp.bfloat16), 'dp').astype(jnp.float32)  235 us
    reduce_scatter x1, waiting for transfers between devices, per_device(): lax.psum_scatter(in_local, ('dp', 'mp'), scatter_dimension=0, tiled=True)  158 us
    psum x1, waiting for transfers between devices, per_device(): lax.psum(jnp.dot(hidden, down_proj, preferred_element_type=jnp.float32).a...  134 us
    reduce_scatter x1, waiting for transfers between devices, per_device(): lax.psum_scatter(out_local, ('dp', 'mp'), scatter_dimension=0, tiled=True)  134 us
    unnamed x2, blocking collectives  82.6 us
    unnamed x10, waiting for transfers between devices  52 us
    dot_general x5, matrix products, inner_cols(): lax.dot_general(left, right, (((1,), (1,)), ((), ())), preferred_element_...  43.7 us
    all_gather x1, blocking collectives, per_device(): lax.all_gather(conv_kernel, ('dp', 'mp'), axis=0, tiled=True)  40.8 us
  transfers between devices with their start and end apart: 12, of which 10 were waited for; matrix products, arithmetic and copies ran while one was open for 9% of the time, Pallas kernels for 0%

commit v1 on v0

--- a/solution.py
+++ b/solution.py
@@ -5,6 +5,10 @@
 
 KERNEL = 3
 epsilon = 1e-05
+
+
+def bind_plate(field):
+    return lax.all_gather(field, axis_name="dp").sum(axis=0)
 
 
 def from_behind(block, axis, distance):
@@ -132,7 +136,7 @@
     input_part, first_local = first_pull(first_grad)
     input_grad = (residual_grad + input_part).reshape(1, row_count, features)
     grad_gate, grad_up, grad_down = (
-        lax.psum(gate_local.astype(jnp.bfloat16), "dp").astype(jnp.float32),
+        bind_plate(gate_local.astype(jnp.bfloat16)).astype(jnp.float32),
         lax.psum(up_local.astype(jnp.bfloat16), "dp").astype(jnp.float32),
         lax.psum(down_local.astype(jnp.bfloat16), "dp").astype(jnp.float32),
     )

time: 1110 us -> 1410 us (1.27)
  waiting for transfers between devices: 795 us -> 1080 us
    all_gather x0 -> x1, waiting for transfers between devices: none -> 357 us  [bind_plate(): return lax.all_gather(field, axis_name='dp').sum(axis=0)]
    psum x1, waiting for transfers between devices: 235 us -> 169 us  [per_device(): lax.psum(up_local.astype(jnp.bfloat16), 'dp').astype(jnp.float32)]
    unnamed x10 -> x11, waiting for transfers between devices: 52 us -> 41.7 us
  transfers between devices with their start and end apart: 12 -> 13, of which waited for: 10 -> 11; matrix products, arithmetic and copies ran while one was open for 9% -> 8% of each run, Pallas kernels for 0% -> 0%
where the time goes in v1:
time: 1410 us; the launch traced here: 1400 us
  waiting for transfers between devices  1080 us (77%)
  blocking collectives  124 us (9%)
  matrix products  119 us (8%)
  other arithmetic  46 us (3%)
  between operations  14.8 us (1%)
    all_gather x1, waiting for transfers between devices, bind_plate(): return lax.all_gather(field, axis_name='dp').sum(axis=0)  357 us
    psum x1, waiting for transfers between devices, per_device(): lax.psum(up_local.astype(jnp.bfloat16), 'dp').astype(jnp.float32)  169 us
    reduce_scatter x1, waiting for transfers between devices, per_device(): lax.psum_scatter(in_local, ('dp', 'mp'), scatter_dimension=0, tiled=True)  159 us
    psum x1, waiting for transfers between devices, per_device(): lax.psum(jnp.dot(hidden, down_proj, preferred_element_type=jnp.float32).a...  143 us
    reduce_scatter x1, waiting for transfers between devices, per_device(): lax.psum_scatter(out_local, ('dp', 'mp'), scatter_dimension=0, tiled=True)  128 us
    unnamed x2, blocking collectives  83 us
    dot_general x5, matrix products, inner_cols(): lax.dot_general(left, right, (((1,), (1,)), ((), ())), preferred_element_...  43.7 us
    unnamed x11, waiting for transfers between devices  41.7 us
  transfers between devices with their start and end apart: 13, of which 11 were waited for; matrix products, arithmetic and copies ran while one was open for 8% of the time, Pallas kernels for 0%

profile of v1, /device:TPU:0, one launch (start us, length us, event | category | flops | bytes accessed | tf_op | source)
XLA Modules:
  0.0 1402.9 jit_solution(2486647343678046684)
XLA Ops:
  7.2 0.7 all-gather.9.cloned.1.call-update
  8.0 0.7 all-gather.11.cloned.1.call-update
  8.7 0.7 convert_element_type.91
  9.5 2.3 collective-permute-start
  11.9 0.8 dynamic-update-slice
  12.7 0.8 dynamic-update-slice.1
  13.5 41.9 %all-reduce.12 = (bf16[1024]{0:T(1024)(128)(2,1)S(1)}, bf16[1024]{0:T(1024)(128)(2,1)S(1)}) all-reduce(bf16[1024]{0:T(1024)(128)(2,1)S(1)} %dynamic-update-slice, bf16[1024]{0:T(1024)(128)(2,1)S(1)} %dynamic-update-slice.1), channel_id=1, replica_groups=mesh['dp'=8,'mp'=4] {'dp','mp'}, use_global_device_ids=true, to_apply=%add.7 | all-reduce | flops 2048 | bytes 8192
  55.4 40.6 %all-gather.2 = bf16[32,32,3]{1,2,0:T(4,128)(2,1)S(1)} all-gather(bf16[1,32,3]{1,2,0:T(4,128)(2,1)} %bitcast.76), channel_id=1, replica_groups=mesh['dp'=8,'mp'=4] {'dp','mp'}, dimensions={0}, use_global_device_ids=true | all-gather | bytes 6336 | tf_op jit(solution)/shard_map/all_gather | solution.py:74
  96.1 1.5 fusion.24
  97.7 6.0 fusion.35
  103.8 0.4 slice_multiply_fusion
  104.2 2.2 collective-permute-start.1
  106.5 0.7 collective-permute-done.1
  107.2 2.5 multiply_convert_fusion.6
  109.7 31.6 %all-gather.11.cloned.1.call-done = bf16[1024,1024]{1,0:T(8,128)(2,1)} async-done(((bf16[32,1024]{1,0:T(8,128)(2,1)}), bf16[1024,1024]{1,0:T(8,128)(2,1)}) %all-gather.11.cloned.1.call-update) | async-done | bytes 2097168 | tf_op jit(solution)/shard_map/all_gather | solution.py:75
  141.3 3.3 multiply_reduce_fusion.3
  144.6 1.4 copy-done.7
  146.0 1.2 multiply_convert_fusion.5
  147.2 0.5 all-gather.15.cloned.1.call-update
  147.8 0.6 all-reduce.20.cloned.1.call-start
  148.3 32.3 %all-gather.13.cloned.1.call-done = bf16[2048,1024]{1,0:T(8,128)(2,1)} async-done(((bf16[512,1024]{1,0:T(8,128)(2,1)}), bf16[2048,1024]{1,0:T(8,128)(2,1)}) %all-gather.13.cloned.1.call-update) | async-done | bytes 4194320 | tf_op jit(solution)/shard_map/all_gather | solution.py:99
  180.7 10.6 fusion.42
  191.3 7.9 fusion.43
  199.2 17.5 %all-gather.15.cloned.1.call-done = bf16[1,2048,1024]{2,1,0:T(8,128)(2,1)} async-done(((bf16[1,512,1024]{2,1,0:T(8,128)(2,1)}), bf16[1,2048,1024]{2,1,0:T(8,128)(2,1)}) %all-gather.15.cloned.1.call-update) | async-done | bytes 4194320 | tf_op jit(solution)/shard_map/all_gather | solution.py:111
  216.6 18.2 %multiply_convert_fusion = (bf16[2048,1152]{1,0:T(8,128)(2,1)}, bf16[2048,1152]{1,0:T(8,128)(2,1)}, bf16[2048,1152]{1,0:T(8,128)(2,1)}) fusion(f32[2048,1152]{1,0:T(8,128)} %fusion.42, f32[2048,1152]{1,0:T(8,128)} %fusion.43, bf16[1152,1024]{1,0:T(8,128)(2,1)S(1)} %copy-done, bf16[1,2048,1024]{2,1,0:T(8,128)(2,1)} %all-gather.15.cloned.1.call-done), kind=kOutput, calls=%fused_computation.4 | convolution fusion | flops 4869586944 | bytes 39583744 | tf_op jit(solution)/shard_map/dot_general | solution.py:35
  234.9 7.7 fusion.44
  242.6 7.1 convolution_convert_fusion.2
  249.7 7.7 add_convert_fusion
  257.5 10.0 convolution_convert_fusion
  267.5 143.3 %all-reduce.20.cloned.1.call-done = (bf16[2048,1024]{1,0:T(8,128)(2,1)}, bf16[2048,1024]{1,0:T(8,128)(2,1)}) async-done(((bf16[2048,1024]{1,0:T(8,128)(2,1)}, bf16[2048,1024]{1,0:T(8,128)(2,1)}), (bf16[2048,1024]{1,0:T(8,128)(2,1)}, bf16[2048,1024]{1,0:T(8,128)(2,1)})) %all-reduce.20.cloned.1.call-update) | async-done | bytes 8388624 | tf_op jit(solution)/shard_map/psum | solution.py:105
  410.8 2.0 fusion.20
  412.9 3.4 fusion.21
  416.3 1.3 fusion.32
  417.6 1.0 copy-done.4
  418.6 0.6 copy-done.10
  419.3 3.7 multiply_reduce_fusion.1
  423.0 1.1 copy.24
  424.1 9.3 fusion.8
  433.5 10.1 convolution_convert_fusion.1
  443.7 1.5 copy-done.6
  445.2 4.5 fusion.30
  449.8 2.0 multiply_select_fusion.2
  451.8 1.6 collective-permute-start.2
  453.4 1.0 pad_add_fusion
  454.4 0.8 collective-permute-done.2
  455.2 0.8 multiply_convert_fusion.4
  456.1 1.0 copy-done.12
  457.0 0.3 copy-done.13
  457.3 6.8 fusion.27
  464.2 8.8 fusion.18
  473.0 41.1 %all-reduce.11 = (f32[1024]{0:T(1024)S(1)}, f32[1024]{0:T(1024)S(1)}) all-reduce(f32[1024]{0:T(1024)S(1)} %get-tuple-element.15, f32[1024]{0:T(1024)S(1)} %get-tuple-element.10), channel_id=4, replica_groups=mesh['dp'=8,'mp'=4] {'dp','mp'}, use_global_device_ids=true, to_apply=%region_7.8.clone | all-reduce | flops 2048 | bytes 16384
  514.1 0.6 dynamic-slice
  514.7 0.6 dynamic-slice.1
  515.3 3.4 fusion.23
  518.7 39.7 %reduce-scatter.10.cloned.1.call-done = f32[32,3]{1,0:T(8,128)} async-done(((f32[1024,3]{1,0:T(8,128)}), f32[32,3]{1,0:T(8,128)}) %reduce-scatter.10.cloned.1.call-update) | async-done | bytes 400
  558.4 1.4 copy.25
  559.8 169.4 %all-reduce.18.cloned.1.call-done = (bf16[1024,1152]{1,0:T(8,128)(2,1)}, bf16[1152,1024]{1,0:T(8,128)(2,1)}) async-done(((bf16[1024,1152]{1,0:T(8,128)(2,1)}, bf16[1152,1024]{1,0:T(8,128)(2,1)}), (bf16[1024,1152]{1,0:T(8,128)(2,1)}, bf16[1152,1024]{1,0:T(8,128)(2,1)})) %all-reduce.18.cloned.1.call-update) | async-done | bytes 4718608 | tf_op jit(solution)/shard_map/psum | solution.py:140
  729.1 4.3 convert_element_type.110
  733.4 2.7 convert_element_type.112
  736.1 356.6 %all-gather.17.cloned.1.call-done = bf16[8192,1152]{1,0:T(8,128)(2,1)} async-done(((bf16[1024,1152]{1,0:T(8,128)(2,1)}), bf16[8192,1152]{1,0:T(8,128)(2,1)}) %all-gather.17.cloned.1.call-update) | async-done | bytes 18874384 | tf_op jit(solution)/shard_map/all_gather | solution.py:11
  1092.8 12.0 reduce_sum.107
  1104.8 4.2 convert_element_type.108
  1108.9 128.1 %reduce-scatter.8.cloned.1.call-done = f32[32,1024]{1,0:T(8,128)} async-done(((f32[1024,1024]{1,0:T(8,128)}), f32[32,1024]{1,0:T(8,128)}) %reduce-scatter.8.cloned.1.call-update) | async-done | bytes 131088 | tf_op jit(solution)/shard_map/reduce_scatter | solution.py:147
  1237.1 158.8 %reduce-scatter.6.cloned.1.call-done = f32[32,3072]{1,0:T(8,128)} async-done(((f32[1024,3072]{1,0:T(8,128)}), f32[32,3072]{1,0:T(8,128)}) %reduce-scatter.6.cloned.1.call-update) | async-done | bytes 393232 | tf_op jit(solution)/shard_map/reduce_scatter | solution.py:145
  (83 shorter events, 1.0 us)
Async XLA Ops:
  7.2 209.4 %copy-start = (bf16[1152,1024]{1,0:T(8,128)(2,1)S(1)}, bf16[1152,1024]{1,0:T(8,128)(2,1)}, u32[]{:S(2)}) copy-start(bf16[1152,1024]{1,0:T(8,128)(2,1)} %param.20) | copy-start | bytes 7077892
  7.2 90.5 %all-gather.9.cloned.1.call-start = ((), (), s32[]{:S(2)}) async-start(), calls=%async_computation.3 | async-start | bytes 6488064 | tf_op jit(solution)/shard_map/all_gather | solution.py:73
  7.9 133.4 %all-gather.11.cloned.1.call-start = ((), (), s32[]{:S(2)}) async-start(), calls=%async_computation.4 | async-start | bytes 2162688 | tf_op jit(solution)/shard_map/all_gather | solution.py:75
  8.7 172.0 %all-gather.13.cloned.1.call-start = ((), (), s32[]{:S(2)}) async-start(), calls=%async_computation.5 | async-start | bytes 5242880 | tf_op jit(solution)/shard_map/all_gather | solution.py:99
  9.5 88.2 %collective-permute-start = (f32[2]{0:T(128)S(1)}, f32[2]{0:T(128)S(1)}, u32[]{:S(2)}, u32[]{:S(2)}) collective-permute-start(f32[2]{0:T(128)S(1)} %slice_bitcast_fusion), channel_id=1, source_target_pairs={{0,1},{1,2},{2,3},{4,5},{5,6},{6,7},{8,9},{9,10},{10,11},{12,13},{... | collective-permute-start | bytes 32 | tf_op jit(solution)/shard_map/ppermute | solution.py:17
  103.8 3.5 copy-start.2
  104.2 3.1 copy-start.3
  104.2 3.0 collective-permute-start.1
  107.2 34.1 %copy-start.9 = (bf16[1,512,1024]{2,1,0:T(8,128)(2,1)S(1)}, bf16[1,512,1024]{2,1,0:T(8,128)(2,1)}, u32[]{:S(2)}) copy-start(bf16[1,512,1024]{2,1,0:T(8,128)(2,1)} %param.11) | copy-start | bytes 3145732
  144.6 1.4 copy-start.7
  147.2 69.4 %all-gather.15.cloned.1.call-start = ((), (), s32[]{:S(2)}) async-start(), calls=%async_computation.8 | async-start | bytes 5242880 | tf_op jit(solution)/shard_map/all_gather | solution.py:111
  147.8 263.1 %all-reduce.20.cloned.1.call-start = ((), (), s32[]{:S(2)}) async-start(), calls=%async_computation.12 | async-start | bytes 16777216 | tf_op jit(solution)/shard_map/psum | solution.py:105
  180.7 10.6 copy-start.16
  180.7 10.6 copy-start.18
  216.6 18.2 %copy-start.17 = (bf16[1024,1152]{1,0:T(8,128)(2,1)S(1)}, bf16[1024,1152]{1,0:T(8,128)(2,1)}, u32[]{:S(2)}) copy-start(bf16[1024,1152]{1,0:T(8,128)(2,1)} %param.18) | copy-start | bytes 7077892
  234.9 7.7 copy-start.21
  234.9 14.8 %slice-start.2 = ((s8[4718592]{0:T(1024)(128)(4,1)}), s8[4194304]{0:T(1024)(128)(4,1)S(1)}, s32[]{:S(2)}) async-start(s8[4718592]{0:T(1024)(128)(4,1)} %bitcast.77), calls=%async_computation.15 | async-start | bytes 8388608
  242.5 7.2 slice-start.3
  242.6 7.1 copy-start.19
  257.4 301.0 %reduce-scatter.10.cloned.1.call-start = ((), (), s32[]{:S(2)}) async-start(), calls=%async_computation.10 | async-start | bytes 540672
  257.5 153.3 %copy-start.8 = (f32[512,1024]{1,0:T(8,128)S(1)}, f32[512,1024]{1,0:T(8,128)}, u32[]{:S(2)}) copy-start(f32[512,1024]{1,0:T(8,128)} %copy-done.7) | copy-start | bytes 6291460
  410.8 2.0 copy-start.14
  412.9 3.4 copy-start.20
  416.3 1.3 copy-start.5
  416.3 2.3 copy-start.4
  416.3 3.0 copy-start.10
  424.0 305.1 %all-reduce.18.cloned.1.call-start = ((), (), s32[]{:S(2)}) async-start(), calls=%async_computation.11 | async-start | bytes 9437184 | tf_op jit(solution)/shard_map/psum | solution.py:140
  433.4 659.3 %all-gather.17.cloned.1.call-start = ((), (), s32[]{:S(2)}) async-start(), calls=%async_computation.9 | async-start | bytes 21233664 | tf_op jit(solution)/shard_map/all_gather | solution.py:11
  443.6 1.6 copy-start.6
  443.6 793.4 %reduce-scatter.8.cloned.1.call-start = ((), (), s32[]{:S(2)}) async-start(), calls=%async_computation.7 | async-start | bytes 4325376 | tf_op jit(solution)/shard_map/reduce_scatter | solution.py:147
  449.7 946.1 %reduce-scatter.6.cloned.1.call-start = ((), (), s32[]{:S(2)}) async-start(), calls=%async_computation.6 | async-start | bytes 12976128 | tf_op jit(solution)/shard_map/reduce_scatter | solution.py:145
  451.8 3.4 slice-start
  451.8 3.3 slice-start.1
  451.8 3.3 collective-permute-start.2
  454.4 3.0 copy-start.11
  456.0 1.0 copy-start.12
  456.0 1.3 copy-start.13
  729.1 4.3 copy-start.15
  1092.8 303.0 %copy-start.1 = (bf16[1152,1024]{1,0:T(8,128)(2,1)S(1)}, bf16[1152,1024]{1,0:T(8,128)(2,1)}, u32[]{:S(2)}) copy-start(bf16[1152,1024]{1,0:T(8,128)(2,1)} %param.20) | copy-start | bytes 7077892
Sparse Core Ops, SparseCore 0:
  10.9 72.5 all-gather.8
  86.4 54.8 all-gather.10
  147.3 33.3 all-gather.12
  182.1 34.4 all-gather.14
  257.6 153.2 all-reduce.19
  424.2 134.1 reduce-scatter.9
  563.0 166.0 all-reduce.17
  731.3 361.4 all-gather.16
  1095.7 141.2 reduce-scatter.7
  1244.5 151.2 reduce-scatter.5
